TPU v7x, 32 devices: a whole 2x2x4 slice. The times are simulated.
32 devices in a mesh: grid: 4 (over z), band: 4 (over y, x), atom: 2 (over core).
Axes of the slice: x: 2, y: 2, z: 4, core: 2. Of those that a mesh axis runs over, the one named last changes fastest.
Arguments:
- psi: float32 [256, 64, 1024], P('band', 'grid'), may hold values from -27 to 27
- potential: float32 [64, 1024], P(('grid', 'atom')), may hold values from -12 to 12
- projectors: float32 [128, 4, 512], P('grid'), may hold values from -5 to 5
- strength: float32 [128, 4], P('grid'), may hold values from 0.5 to 8
- sphere_index: int32 [128, 512], P('grid'), may hold values from 2048 to 25599, as said below
- atom_count: int32 [4], P('grid'), may hold values from 2 to 32, as said below
Outputs:
- orthonormal: float32 [256, 64, 1024], P('band', ('grid', 'atom'))
Inputs may be any that keep to these rules, and one draw needn't show every extreme that they name: `sphere_index`: row a lists the 512 cells of an 8 x 8 x 8 cube about the atom's centre, offsets -4 to 3 in each direction, as e * 1024 + x * 32 + y with e counted from 6 rows below its domain. `atom_count`: the live slots of a domain are its first ones; in every draw some domain has all 32 live.
All inputs are finite; a program needn't handle non-finite values.
Results may differ from a plain program's by a relative error of at most 0.0003.
Values sent between devices are 32-bit elements; how exact they have to be, the bound alone decides.
A program may use at most 128 MiB of HBM per device.

v0:
```python
import math
import jax
import jax.numpy as jnp
from jax import lax
from jax.sharding import PartitionSpec as P

BANDS = 256
CY = 32
STENCIL = (
    -5369.0 / 1800.0,
    12.0 / 7.0,
    -15.0 / 56.0,
    10.0 / 189.0,
    -1.0 / 112.0,
    2.0 / 1925.0,
    -1.0 / 16632.0,
)
KINETIC = -0.5 * 4.0
STEP_SIZE = 0.05
HIGHEST = lax.Precision.HIGHEST


def from_behind(block, axis, distance):
    devices = range(lax.axis_size(axis))
    route = [((i - distance) % len(devices), i) for i in devices]
    return lax.ppermute(block, axis, route)


def extended_2(x, sides, width):
    for axis, dim in sides:
        count, length = (lax.axis_size(axis), x.shape[dim])
        up = [(i, (i + 1) % count) for i in range(count)]
        down = [(j, i) for i, j in up]
        last = lax.slice_in_dim(x, length - width, length, axis=dim)
        first = lax.slice_in_dim(x, 0, width, axis=dim)
        before = lax.ppermute(last, axis, up)
        after = lax.ppermute(first, axis, down)
        x = jnp.concatenate([before, x, after], axis=dim)
    return x


def inner_rows(left, right):
    return lax.dot_general(
        left, right, (((1,), (1,)), ((), ())), precision=HIGHEST, preferred_element_type=jnp.float32
    )


def spread_terms(weighted, projectors, sphere_index, total_cells):
    band_rows = weighted.shape[0]
    values = jnp.einsum("nai,ais->nas", weighted, projectors, precision=HIGHEST)
    dense = jnp.zeros((band_rows, total_cells), jnp.float32)
    return dense.at[:, sphere_index.reshape(-1)].add(values.reshape(band_rows, -1))


def fold_rims(dense, depth):
    from_below = from_behind(dense[:, depth + 6 :], "grid", 1)
    from_above = from_behind(dense[:, :6], "grid", -1)
    inner = dense[:, 6 : depth + 6]
    inner = inner.at[:, :6].add(from_below)
    return inner.at[:, depth - 6 :].add(from_above)


def body(psi, potential, projectors, strength, sphere_index, atom_count):
    band_rows, depth, plane_cells = psi.shape
    groups = lax.axis_size("atom")
    core = lax.axis_index("atom")
    half = depth // groups
    extended = extended_2(psi, (("grid", 1),), 6)
    window = lax.dynamic_slice_in_dim(extended, core * half, half + 12, 1)
    centre = window[:, 6 : 6 + half]
    margin = 6 * CY
    padded = jnp.pad(centre, ((0, 0), (0, 0), (margin, margin)))
    column = lax.iota(jnp.int32, plane_cells) % CY
    laplace = 3.0 * STENCIL[0] * centre
    for k in range(1, 7):
        along_z = window[:, 6 + k : 6 + k + half] + window[:, 6 - k : 6 - k + half]
        along_x = (
            padded[:, :, margin + k * CY : margin + k * CY + plane_cells]
            + padded[:, :, margin - k * CY : margin - k * CY + plane_cells]
        )
        upper = jnp.where(column + k < CY, padded[:, :, margin + k : margin + k + plane_cells], 0.0)
        lower = jnp.where(column >= k, padded[:, :, margin - k : margin - k + plane_cells], 0.0)
        laplace = laplace + STENCIL[k] * (along_z + along_x + upper + lower)
    atom_slots = sphere_index.shape[0]
    share = atom_slots // groups
    alive_mask = (lax.iota(jnp.int32, atom_slots) < atom_count[0]).astype(jnp.float32)
    scaled = strength * alive_mask[:, None]
    flattened = extended.reshape(band_rows, -1)
    total_cells = flattened.shape[1]
    own_index = lax.dynamic_slice_in_dim(sphere_index, core * share, share, 0)
    own_projectors = lax.dynamic_slice_in_dim(projectors, core * share, share, 0)
    own_scaled = lax.dynamic_slice_in_dim(scaled, core * share, share, 0)
    points = flattened[:, own_index]
    intersections = jnp.einsum(
        "nas,ais->nai", points, own_projectors, precision=HIGHEST
    ) / math.sqrt(projectors.shape[2])
    weighted = intersections * own_scaled[None]
    dense = spread_terms(weighted, own_projectors, own_index, total_cells).reshape(
        band_rows, depth + 12, plane_cells
    )
    nonlocal_half = lax.psum_scatter(
        fold_rims(dense, depth), "atom", scatter_dimension=1, tiled=True
    )
    updated = centre - STEP_SIZE * (KINETIC * laplace + potential * centre + nonlocal_half)
    flat_rows = updated.reshape(band_rows, half * plane_cells)
    cells_total = lax.axis_size("grid") * depth * plane_cells
    block = inner_rows(flat_rows, lax.all_gather(flat_rows, "band", axis=0, tiled=True))
    summed_rows = lax.psum(block, ("grid", "atom")) / cells_total
    intersection_matrix = lax.all_gather(summed_rows, "band", axis=0, tiled=True)
    factor = jnp.linalg.cholesky(intersection_matrix)
    inverse = lax.linalg.triangular_solve(
        factor, jnp.eye(BANDS, dtype=jnp.float32), left_side=True, lower=True
    )
    own_inverse = lax.dynamic_slice_in_dim(
        inverse, lax.axis_index("band") * band_rows, band_rows, 0
    )
    result = jnp.dot(
        own_inverse,
        lax.all_gather(flat_rows, "band", axis=0, tiled=True),
        precision=HIGHEST,
        preferred_element_type=jnp.float32,
    )
    return result.reshape(band_rows, half, plane_cells)


def solution(mesh):
    in_specs = (
        P("band", "grid", None),
        P(("grid", "atom"), None),
        P("grid", None, None),
        P("grid", None),
        P("grid", None),
        P("grid"),
    )
    out_specs = P("band", ("grid", "atom"), None)
    return jax.shard_map(body, mesh=mesh, in_specs=in_specs, out_specs=out_specs, check_vma=False)
```

profile of v0, /device:TPU:0, one launch (start us, length us, event | category | flops | bytes accessed | tf_op | source)
XLA Modules:
  0.0 547.4 jit_solution(13201074883905596832)
XLA Ops:
  6.5 2.7 fusion.95
  9.3 0.9 copy.62
  10.2 3.1 collective-permute-start
  13.3 0.9 copy.63
  14.2 2.4 collective-permute-start.1
  17.4 0.1 fusion.91
  17.5 0.1 copy.43
  17.6 33.1 %collective-permute-done = f32[64,6,1024]{2,0,1:T(8,128)} collective-permute-done((f32[64,6,1024]{2,0,1:T(8,128)S(1)}, f32[64,6,1024]{2,0,1:T(8,128)}, u32[]{:S(2)}, u32[]{:S(2)}) %collective-permute-start) | collective-permute-done | bytes 1572896 | tf_op jit(solution)/shard_map/ppermute | solution.py:36
  50.7 2.7 constant_dynamic-update-slice_fusion.2
  53.5 6.6 %constant_dynamic-update-slice_fusion.1 = f32[64,28,1024]{2,0,1:T(8,128)} fusion(f32[64,28,1024]{2,0,1:T(8,128)} %constant_dynamic-update-slice_fusion.2, f32[64,16,1024]{2,1,0:T(8,128)} %param.10), kind=kLoop, calls=%fused_computation.132 | loop fusion | bytes 8388608
  60.1 23.5 %collective-permute-done.1 = f32[64,6,1024]{2,0,1:T(8,128)} collective-permute-done((f32[64,6,1024]{2,0,1:T(8,128)S(1)}, f32[64,6,1024]{2,0,1:T(8,128)}, u32[]{:S(2)}, u32[]{:S(2)}) %collective-permute-start.1) | collective-permute-done | bytes 1572896 | tf_op jit(solution)/shard_map/ppermute | solution.py:37
  83.5 2.8 constant_dynamic-update-slice_fusion
  86.4 11.1 %copy.41 = f32[64,28,1024]{0,2,1:T(8,128)} copy(f32[64,28,1024]{2,0,1:T(8,128)} %constant_dynamic-update-slice_fusion) | data formatting | bytes 14680064 | tf_op jit(solution)/shard_map/concatenate | solution.py:38
  97.5 32.9 %gather_fusion = f32[8192,64]{1,0:T(8,128)} fusion(f32[64,28672]{0,1:T(8,128)} %bitcast.71, s32[8192]{0:T(1024)S(1)} %broadcast_clamp_fusion), kind=kCustom, calls=%fused_computation | custom fusion | bytes 4227072 | tf_op jit(solution)/shard_map/gather | solution.py:93
  130.4 2.8 copy.42
  133.2 1.8 fusion.62
  135.1 1.9 convolution_bitcast_fusion
  136.9 0.2 copy.56
  137.2 2.7 copy.45
  139.9 50.9 %scatter_custom_fusion = f32[64,28672]{0,1:T(8,128)} fusion(s32[8192]{0:T(1024)S(1)} %bitcast.79, f32[8192,64]{1,0:T(8,128)} %copy.45, f32[]{:T(128)} %constant.181.clone.1), kind=kCustom, calls=%fused_computation.28 | custom fusion | flops 524288 | bytes 7340544 | tf_op jit(solution)/shard_map/scatter-add | solution.py:52
  190.8 7.1 %fusion.94 = (f32[64,6,1024]{0,2,1:T(8,128)}, f32[64,6,1024]{0,2,1:T(8,128)}, f32[64,6,1024]{0,2,1:T(8,128)S(1)}) fusion(f32[64,28,1024]{0,2,1:T(8,128)} %bitcast.69), kind=kLoop, calls=%fused_computation.166 | loop fusion | bytes 9437184 | tf_op jit(solution)/shard_map/slice | solution.py:57
  197.8 3.2 copy.54
  201.1 0.6 collective-permute-start.2
  201.6 3.2 copy.55
  204.9 10.5 %collective-permute-start.3 = (f32[64,6,1024]{2,0,1:T(8,128)}, f32[64,6,1024]{2,0,1:T(8,128)}, u32[]{:S(2)}, u32[]{:S(2)}) collective-permute-start(f32[64,6,1024]{2,0,1:T(8,128)} %copy.55), channel_id=1, source_target_pairs={{8,0},{16,8},{24,16},{0,24},{9,1},{17,9},{25,17},{1,25},{10,2},{18... | collective-permute-start | bytes 4718600 | tf_op jit(solution)/shard_map/ppermute | solution.py:26
  215.4 7.5 %slice.277 = f32[64,16,1024]{0,2,1:T(8,128)} slice(f32[64,28,1024]{0,2,1:T(8,128)} %bitcast.70), slice={[0:64], [6:22], [0:1024]} | slice | bytes 8388608 | tf_op jit(solution)/shard_map/slice | solution.py:58
  222.8 2.0 copy.53
  224.9 6.9 %copy.52 = f32[64,16,1024]{2,0,1:T(8,128)} copy(f32[64,16,1024]{0,2,1:T(8,128)} %slice.277) | data formatting | bytes 8388608
  231.8 16.0 %collective-permute-done.2 = f32[64,6,1024]{2,0,1:T(8,128)} collective-permute-done((f32[64,6,1024]{2,0,1:T(8,128)}, f32[64,6,1024]{2,0,1:T(8,128)}, u32[]{:S(2)}, u32[]{:S(2)}) %collective-permute-start.2) | collective-permute-done | bytes 1572896 | tf_op jit(solution)/shard_map/ppermute | solution.py:26
  247.7 2.8 add_dynamic-update-slice_fusion
  250.6 22.7 %collective-permute-done.3 = f32[64,6,1024]{2,0,1:T(8,128)} collective-permute-done((f32[64,6,1024]{2,0,1:T(8,128)}, f32[64,6,1024]{2,0,1:T(8,128)}, u32[]{:S(2)}, u32[]{:S(2)}) %collective-permute-start.3) | collective-permute-done | bytes 1572896 | tf_op jit(solution)/shard_map/ppermute | solution.py:26
  273.2 3.4 fusion.58
  276.6 0.0 reduce-scatter.2.cloned.1.call-update
  276.7 0.0 all-gather.2.cloned.1.call-start
  276.8 1.7 constant_dynamic-slice_fusion.1
  278.5 8.5 %reduce-scatter.2.cloned.1.call-done = f32[64,8,1024]{2,0,1:T(8,128)} async-done(((f32[64,16,1024]{2,0,1:T(8,128)}), f32[64,8,1024]{2,0,1:T(8,128)}) %reduce-scatter.2.cloned.1.call-update) | async-done | bytes 2097168 | tf_op jit(solution)/shard_map/reduce_scatter | solution.py:101
  287.1 15.7 %fusion.57 = f32[8,8,8,1024]{3,2,1,0:T(8,128)S(1)} fusion(f32[64,8,1024]{2,0,1:T(8,128)S(1)} %constant_dynamic-slice_fusion.1, f32[64,8,1024]{2,0,1:T(8,128)} %reduce-scatter.2.cloned.1.call-done, f32[64,28,1024]{2,0,1:T(8,128)} %constant_dynamic-update-slice_fusion, s32[]{:T(128)S(6)} %select_n.94, s32[]{:T(128)S(6)} %add.301, s32[]{:T(128)S(6)} %add.300, ...), kind=kLoop, calls=%fused_computation.91 | loop fusion | flops 31981568 | bytes 31502384
  302.8 1.6 copy.57
  304.4 0.0 all-reduce.4.cloned.1.call-start
  304.5 88.8 %all-gather.2.cloned.1.call-done = f32[256,8192]{1,0:T(8,128)} async-done(((f32[64,8192]{1,0:T(8,128)}), f32[256,8192]{1,0:T(8,128)}) %all-gather.2.cloned.1.call-update) | async-done | bytes 8388624 | tf_op jit(solution)/shard_map/all_gather | solution.py:107
  393.3 10.7 %fusion.96 = f32[64,256]{1,0:T(8,128)} fusion(f32[64,8192]{1,0:T(8,128)S(1)} %bitcast.73, f32[256,8192]{1,0:T(8,128)} %all-gather.2.cloned.1.call-done), kind=kOutput, calls=%fused_computation.168 | convolution fusion | flops 1610612736 | bytes 10551296 | tf_op jit(solution)/shard_map/dot_general | solution.py:43
  404.1 54.8 %all-reduce.4.cloned.1.call-done = f32[64,256]{1,0:T(8,128)} async-done(((f32[64,256]{1,0:T(8,128)}), f32[64,256]{1,0:T(8,128)}) %all-reduce.4.cloned.1.call-update) | async-done | bytes 65552 | tf_op jit(solution)/shard_map/psum | solution.py:108
  458.9 0.8 broadcast_multiply_fusion
  459.7 9.4 %all_gather.8 = f32[256,256]{1,0:T(8,128)S(1)} all-gather(f32[64,256]{1,0:T(8,128)S(1)} %broadcast_multiply_fusion), channel_id=1, replica_groups=mesh['grid'=4,'band'=4,'atom'=2] {'band'}, dimensions={0}, use_global_device_ids=true | all-gather | bytes 327680 | tf_op jit(solution)/shard_map/all_gather | solution.py:109
  469.2 0.1 copy.51
  469.4 11.7 %cholesky.50 = f32[128,128]{1,0:T(8,128)S(1)} custom-call(f32[128,128]{1,0:T(8,128)S(1)} %cholesky.118), custom_call_target="Cholesky" | custom-call | tf_op jit(solution)/shard_map/jit(cholesky)/cholesky | solution.py:110
  481.2 9.8 %custom-call.14 = f32[1,128,128]{1,2,0:T(8,128)S(1)} custom-call(f32[1,128,128]{2,1,0:T(8,128)S(1)} %get-tuple-element.55), custom_call_target="InvertDiagBlocksLowerTriangular" | custom-call | tf_op jit(solution)/shard_map/jit(cholesky)/cholesky | solution.py:110
  491.0 0.2 constant_dynamic-update-slice_fusion.3
  491.2 0.3 convolution_subtract_fusion.1
  491.4 11.7 %cholesky.105 = f32[128,128]{1,0:T(8,128)S(1)} custom-call(f32[128,128]{1,0:T(8,128)S(1)} %convolution_subtract_fusion.1), custom_call_target="Cholesky" | custom-call | tf_op jit(solution)/shard_map/jit(cholesky)/cholesky | solution.py:110
  503.2 0.7 compare_reduce_fusion
  503.9 0.6 compare_reduce_fusion.1
  505.8 0.1 triangular_solve.63
  505.9 4.1 while.3
  506.1 0.6 fusion.106
  506.7 1.4 bitcast_dynamic-update-slice_fusion.2
  508.1 0.6 fusion.106
  508.7 1.4 bitcast_dynamic-update-slice_fusion.2
  510.1 19.7 %custom-call.15 = f32[2,128,128]{1,2,0:T(8,128)S(1)} custom-call(f32[2,128,128]{2,1,0:T(8,128)S(1)} %get-tuple-element.36), custom_call_target="InvertDiagBlocksLowerTriangular" | custom-call | tf_op jit(solution)/shard_map/triangular_solve | solution.py:111
  529.7 0.3 fusion.66
  530.0 0.3 convolution_subtract_fusion
  530.3 0.3 fusion.74
  530.6 7.5 %fusion.71 = f32[64,8192]{1,0:T(8,128)S(1)} fusion(f32[256,8192]{1,0:T(8,128)} %all-gather.2.cloned.1.call-done, s32[]{:T(128)S(6)} %select_n.112, f32[128,256]{1,0:T(8,128)S(1)} %fusion.66, f32[128,256]{1,0:T(8,128)S(1)} %fusion.74), kind=kOutput, calls=%fused_computation.114 | convolution fusion | flops 1610629120 | bytes 10747908 | tf_op jit(solution)/shard_map/dot_general | solution.py:117
  538.1 2.5 copy.60
  (41 shorter events, 0.4 us)
Async XLA Ops:
  6.5 126.7 %copy-start = (f32[32,4,512]{2,1,0:T(4,128)S(1)}, f32[32,4,512]{2,1,0:T(4,128)}, u32[]{:S(2)}) copy-start(f32[32,4,512]{2,1,0:T(4,128)} %param.12) | copy-start | bytes 786436
  6.5 280.5 %reduce-scatter.2.cloned.1.call-start = ((), (), s32[]{:S(2)}) async-start(), calls=%async_computation.1 | async-start | bytes 6291456 | tf_op jit(solution)/shard_map/reduce_scatter | solution.py:101
  10.2 6.4 %copy-start.5 = (s32[32,512]{1,0:T(8,128)S(1)}, s32[32,512]{1,0:T(8,128)}, u32[]{:S(2)}) copy-start(s32[32,512]{1,0:T(8,128)} %param.14) | copy-start | bytes 196612
  10.2 7.2 %copy-start.6 = (f32[32,4]{0,1:T(4,128)S(1)}, f32[32,4]{0,1:T(4,128)}, u32[]{:S(2)}) copy-start(f32[32,4]{0,1:T(4,128)} %param.13) | copy-start | bytes 1540
  10.2 40.5 %collective-permute-start = (f32[64,6,1024]{2,0,1:T(8,128)S(1)}, f32[64,6,1024]{2,0,1:T(8,128)}, u32[]{:S(2)}, u32[]{:S(2)}) collective-permute-start(f32[64,6,1024]{2,0,1:T(8,128)S(1)} %copy.62), channel_id=1, source_target_pairs={{0,8},{8,16},{16,24},{24,0},{1,9},{9,17},{17,25},{25,1},{2,10},{10... | collective-permute-start | bytes 4718600 | tf_op jit(solution)/shard_map/ppermute | solution.py:36
  14.2 69.3 %collective-permute-start.1 = (f32[64,6,1024]{2,0,1:T(8,128)S(1)}, f32[64,6,1024]{2,0,1:T(8,128)}, u32[]{:S(2)}, u32[]{:S(2)}) collective-permute-start(f32[64,6,1024]{2,0,1:T(8,128)S(1)} %copy.63), channel_id=1, source_target_pairs={{8,0},{16,8},{24,16},{0,24},{9,1},{17,9},{25,17},{1,25},{10,2},{18... | collective-permute-start | bytes 4718600 | tf_op jit(solution)/shard_map/ppermute | solution.py:37
  201.1 46.6 %collective-permute-start.2 = (f32[64,6,1024]{2,0,1:T(8,128)}, f32[64,6,1024]{2,0,1:T(8,128)}, u32[]{:S(2)}, u32[]{:S(2)}) collective-permute-start(f32[64,6,1024]{2,0,1:T(8,128)} %copy.54), channel_id=1, source_target_pairs={{24,0},{0,8},{8,16},{16,24},{25,1},{1,9},{9,17},{17,25},{26,2},{2,... | collective-permute-start | bytes 4718600 | tf_op jit(solution)/shard_map/ppermute | solution.py:26
  204.9 68.4 %collective-permute-start.3 = (f32[64,6,1024]{2,0,1:T(8,128)}, f32[64,6,1024]{2,0,1:T(8,128)}, u32[]{:S(2)}, u32[]{:S(2)}) collective-permute-start(f32[64,6,1024]{2,0,1:T(8,128)} %copy.55), channel_id=1, source_target_pairs={{8,0},{16,8},{24,16},{0,24},{9,1},{17,9},{25,17},{1,25},{10,2},{18... | collective-permute-start | bytes 4718600 | tf_op jit(solution)/shard_map/ppermute | solution.py:26
  224.9 22.9 %copy-start.3 = (f32[64,6,1024]{2,0,1:T(8,128)S(1)}, f32[64,6,1024]{2,0,1:T(8,128)}, u32[]{:S(2)}) copy-start(f32[64,6,1024]{2,0,1:T(8,128)} %copy.53) | copy-start | bytes 4718596
  276.7 116.6 %all-gather.2.cloned.1.call-start = ((), (), s32[]{:S(2)}) async-start(), calls=%async_computation.2 | async-start | bytes 10485760 | tf_op jit(solution)/shard_map/all_gather | solution.py:107
  276.8 10.3 %copy-start.4 = (f32[8,1024]{1,0:T(8,128)S(1)}, f32[8,1024]{1,0:T(8,128)}, u32[]{:S(2)}) copy-start(f32[8,1024]{1,0:T(8,128)} %param.11) | copy-start | bytes 98308
  304.3 89.0 %copy-start.2 = (f32[8,8,8,1024]{3,2,0,1:T(8,128)S(1)}, f32[8,8,8,1024]{3,2,0,1:T(8,128)}, u32[]{:S(2)}) copy-start(f32[8,8,8,1024]{3,2,0,1:T(8,128)} %copy.57) | copy-start | bytes 6291460
  304.4 154.5 %all-reduce.4.cloned.1.call-start = ((), (), s32[]{:S(2)}) async-start(), calls=%async_computation.3 | async-start | bytes 131072 | tf_op jit(solution)/shard_map/psum | solution.py:108
  538.1 2.5 copy-start.1
Sparse Core Ops, SparseCore 0:
  276.8 10.2 reduce-scatter.1
  304.5 88.7 all-gather.1
  404.2 54.6 all-reduce.3
where the time goes:
time: 551 us; the launch traced here: 547 us
  waiting for transfers between devices  247 us (45%)
  other arithmetic  128 us (23%)
  local copies, waits for them, and re-layouts  107 us (19%)
  matrix products  23.2 us (4%)
  starting transfers between devices  16.7 us (3%)
  between operations  15.6 us (3%)
  blocking collectives  9.45 us (2%)
    all_gather x1, waiting for transfers between devices, body(): lax.all_gather(flat_rows, 'band', axis=0, tiled=True)  88.8 us
    psum x1, waiting for transfers between devices, body(): summed_rows = lax.psum(block, ('grid', 'atom')) / cells_total  54.8 us
    scatter-add x1, other arithmetic, spread_terms(): dense.at[:, sphere_index.reshape(-1)].add(values.reshape(band_rows, -1))  50.9 us
    ppermute x2, waiting for transfers between devices, from_behind(): return lax.ppermute(block, axis, route)  38.6 us
    gather x2, local copies, waits for them, and re-layouts, body(): points = flattened[:, own_index]  35.8 us
    another operation x7, other arithmetic, body(): factor = jnp.linalg.cholesky(intersection_matrix)  34.6 us
    ppermute x1, waiting for transfers between devices, extended_2(): before = lax.ppermute(last, axis, up)  33.1 us
    unnamed x25, local copies, waits for them, and re-layouts  29.1 us
  transfers between devices with their start and end apart: 7, of which 7 were waited for; matrix products, arithmetic and copies ran while one was open for 6% of the time, Pallas kernels for 0%

commit v1 on v0

--- a/solution.py
+++ b/solution.py
@@ -105,7 +105,7 @@
     flat_rows = updated.reshape(band_rows, half * plane_cells)
     cells_total = lax.axis_size("grid") * depth * plane_cells
     block = inner_rows(flat_rows, lax.all_gather(flat_rows, "band", axis=0, tiled=True))
-    summed_rows = lax.psum(block, ("grid", "atom")) / cells_total
+    summed_rows = jnp.sum(lax.all_gather(block, ("grid", "atom")), axis=0) / cells_total
     intersection_matrix = lax.all_gather(summed_rows, "band", axis=0, tiled=True)
     factor = jnp.linalg.cholesky(intersection_matrix)
     inverse = lax.linalg.triangular_solve(

time: 551 us -> 509 us (0.924)
  waiting for transfers between devices: 247 us -> 193 us
  blocking collectives: 9.45 us -> 23.9 us
    psum x1 -> x0, waiting for transfers between devices: 54.8 us -> none  [body(): summed_rows = lax.psum(block, ('grid', 'atom')) / cells_total]
    all_gather x0 -> x1, blocking collectives: none -> 14.7 us  [body(): lax.all_gather(block, ('grid', 'atom'))]
  transfers between devices with their start and end apart: 7 -> 6, of which waited for: 7 -> 6; matrix products, arithmetic and copies ran while one was open for 6% -> 7% of each run, Pallas kernels for 0% -> 0%
where the time goes in v1:
time: 509 us; the launch traced here: 506 us
  waiting for transfers between devices  193 us (38%)
  other arithmetic  127 us (25%)
  local copies, waits for them, and re-layouts  107 us (21%)
  blocking collectives  23.9 us (5%)
  matrix products  22.6 us (4%)
  starting transfers between devices  16.6 us (3%)
  between operations  15.9 us (3%)
    all_gather x1, waiting for transfers between devices, body(): lax.all_gather(flat_rows, 'band', axis=0, tiled=True)  88.9 us
    scatter-add x1, other arithmetic, spread_terms(): dense.at[:, sphere_index.reshape(-1)].add(values.reshape(band_rows, -1))  50.9 us
    ppermute x2, waiting for transfers between devices, from_behind(): return lax.ppermute(block, axis, route)  38.6 us
    gather x2, local copies, waits for them, and re-layouts, body(): points = flattened[:, own_index]  35.9 us
    another operation x7, other arithmetic, body(): factor = jnp.linalg.cholesky(intersection_matrix)  34.6 us
    ppermute x1, waiting for transfers between devices, extended_2(): before = lax.ppermute(last, axis, up)  33.1 us
    unnamed x25, local copies, waits for them, and re-layouts  29.2 us
    ppermute x1, waiting for transfers between devices, extended_2(): after = lax.ppermute(first, axis, down)  23.4 us
  transfers between devices with their start and end apart: 6, of which 6 were waited for; matrix products, arithmetic and copies ran while one was open for 7% of the time, Pallas kernels for 0%

profile of v1, /device:TPU:0, one launch (start us, length us, event | category | flops | bytes accessed | tf_op | source)
XLA Modules:
  0.0 506.0 jit_solution(9715899000092682319)
XLA Ops:
  6.5 2.7 fusion.95
  9.3 0.9 copy.60
  10.2 0.0 copy-start.6
  10.2 3.1 collective-permute-start
  13.3 0.9 copy.61
  14.2 2.4 collective-permute-start.1
  17.4 0.1 fusion.91
  17.5 0.1 copy.41
  17.6 33.1 %collective-permute-done = f32[64,6,1024]{2,0,1:T(8,128)} collective-permute-done((f32[64,6,1024]{2,0,1:T(8,128)S(1)}, f32[64,6,1024]{2,0,1:T(8,128)}, u32[]{:S(2)}, u32[]{:S(2)}) %collective-permute-start) | collective-permute-done | bytes 1572896 | tf_op jit(solution)/shard_map/ppermute | solution.py:36
  50.7 2.7 constant_dynamic-update-slice_fusion.2
  53.5 6.6 %constant_dynamic-update-slice_fusion.1 = f32[64,28,1024]{2,0,1:T(8,128)} fusion(f32[64,28,1024]{2,0,1:T(8,128)} %constant_dynamic-update-slice_fusion.2, f32[64,16,1024]{2,1,0:T(8,128)} %param.10), kind=kLoop, calls=%fused_computation.132 | loop fusion | bytes 8388608
  60.1 23.4 %collective-permute-done.1 = f32[64,6,1024]{2,0,1:T(8,128)} collective-permute-done((f32[64,6,1024]{2,0,1:T(8,128)S(1)}, f32[64,6,1024]{2,0,1:T(8,128)}, u32[]{:S(2)}, u32[]{:S(2)}) %collective-permute-start.1) | collective-permute-done | bytes 1572896 | tf_op jit(solution)/shard_map/ppermute | solution.py:37
  83.5 2.8 constant_dynamic-update-slice_fusion
  86.4 11.1 %copy.39 = f32[64,28,1024]{0,2,1:T(8,128)} copy(f32[64,28,1024]{2,0,1:T(8,128)} %constant_dynamic-update-slice_fusion) | data formatting | bytes 14680064 | tf_op jit(solution)/shard_map/concatenate | solution.py:38
  97.5 33.1 %gather_fusion = f32[8192,64]{1,0:T(8,128)} fusion(f32[64,28672]{0,1:T(8,128)} %bitcast.72, s32[8192]{0:T(1024)S(1)} %broadcast_clamp_fusion), kind=kCustom, calls=%fused_computation | custom fusion | bytes 4227072 | tf_op jit(solution)/shard_map/gather | solution.py:93
  130.5 2.8 copy.40
  133.4 1.8 fusion.62
  135.2 1.9 convolution_bitcast_fusion
  137.1 0.2 copy.54
  137.3 2.7 copy.43
  140.0 50.9 %scatter_custom_fusion = f32[64,28672]{0,1:T(8,128)} fusion(s32[8192]{0:T(1024)S(1)} %bitcast.81, f32[8192,64]{1,0:T(8,128)} %copy.43, f32[]{:T(128)} %constant.181.clone.1), kind=kCustom, calls=%fused_computation.28 | custom fusion | flops 524288 | bytes 7340544 | tf_op jit(solution)/shard_map/scatter-add | solution.py:52
  190.9 7.1 %fusion.94 = (f32[64,6,1024]{0,2,1:T(8,128)}, f32[64,6,1024]{0,2,1:T(8,128)}, f32[64,6,1024]{0,2,1:T(8,128)S(1)}) fusion(f32[64,28,1024]{0,2,1:T(8,128)} %bitcast.70), kind=kLoop, calls=%fused_computation.166 | loop fusion | bytes 9437184 | tf_op jit(solution)/shard_map/slice | solution.py:57
  198.0 3.3 copy.52
  201.3 0.6 collective-permute-start.2
  201.8 3.2 copy.53
  205.1 10.5 %collective-permute-start.3 = (f32[64,6,1024]{2,0,1:T(8,128)}, f32[64,6,1024]{2,0,1:T(8,128)}, u32[]{:S(2)}, u32[]{:S(2)}) collective-permute-start(f32[64,6,1024]{2,0,1:T(8,128)} %copy.53), channel_id=1, source_target_pairs={{8,0},{16,8},{24,16},{0,24},{9,1},{17,9},{25,17},{1,25},{10,2},{18... | collective-permute-start | bytes 4718600 | tf_op jit(solution)/shard_map/ppermute | solution.py:26
  215.6 7.5 %slice.277 = f32[64,16,1024]{0,2,1:T(8,128)} slice(f32[64,28,1024]{0,2,1:T(8,128)} %bitcast.71), slice={[0:64], [6:22], [0:1024]} | slice | bytes 8388608 | tf_op jit(solution)/shard_map/slice | solution.py:58
  223.1 2.0 copy.51
  225.1 6.9 %copy.50 = f32[64,16,1024]{2,0,1:T(8,128)} copy(f32[64,16,1024]{0,2,1:T(8,128)} %slice.277) | data formatting | bytes 8388608
  232.0 15.9 %collective-permute-done.2 = f32[64,6,1024]{2,0,1:T(8,128)} collective-permute-done((f32[64,6,1024]{2,0,1:T(8,128)}, f32[64,6,1024]{2,0,1:T(8,128)}, u32[]{:S(2)}, u32[]{:S(2)}) %collective-permute-start.2) | collective-permute-done | bytes 1572896 | tf_op jit(solution)/shard_map/ppermute | solution.py:26
  247.9 2.8 add_dynamic-update-slice_fusion
  250.8 22.7 %collective-permute-done.3 = f32[64,6,1024]{2,0,1:T(8,128)} collective-permute-done((f32[64,6,1024]{2,0,1:T(8,128)}, f32[64,6,1024]{2,0,1:T(8,128)}, u32[]{:S(2)}, u32[]{:S(2)}) %collective-permute-start.3) | collective-permute-done | bytes 1572896 | tf_op jit(solution)/shard_map/ppermute | solution.py:26
  273.4 3.4 fusion.58
  276.8 0.0 reduce-scatter.2.cloned.1.call-update
  276.9 0.0 all-gather.3.cloned.1.call-start
  277.0 1.7 constant_dynamic-slice_fusion.1
  278.7 8.5 %reduce-scatter.2.cloned.1.call-done = f32[64,8,1024]{2,0,1:T(8,128)} async-done(((f32[64,16,1024]{2,0,1:T(8,128)}), f32[64,8,1024]{2,0,1:T(8,128)}) %reduce-scatter.2.cloned.1.call-update) | async-done | bytes 2097168 | tf_op jit(solution)/shard_map/reduce_scatter | solution.py:101
  287.3 15.7 %fusion.57 = f32[8,8,8,1024]{3,2,1,0:T(8,128)S(1)} fusion(f32[64,8,1024]{2,0,1:T(8,128)S(1)} %constant_dynamic-slice_fusion.1, f32[64,8,1024]{2,0,1:T(8,128)} %reduce-scatter.2.cloned.1.call-done, f32[64,28,1024]{2,0,1:T(8,128)} %constant_dynamic-update-slice_fusion, s32[]{:T(128)S(6)} %select_n.94, s32[]{:T(128)S(6)} %add.299, s32[]{:T(128)S(6)} %add.298, ...), kind=kLoop, calls=%fused_computation.91 | loop fusion | flops 31981568 | bytes 31502384
  303.0 1.6 copy.55
  304.5 0.0 all-gather.3.cloned.1.call-update
  304.6 88.9 %all-gather.3.cloned.1.call-done = f32[256,8192]{1,0:T(8,128)} async-done(((f32[64,8192]{1,0:T(8,128)}), f32[256,8192]{1,0:T(8,128)}) %all-gather.3.cloned.1.call-update) | async-done | bytes 8388624 | tf_op jit(solution)/shard_map/all_gather | solution.py:107
  393.5 10.1 %fusion.96 = f32[64,256]{1,0:T(8,128)S(1)} fusion(f32[64,8192]{1,0:T(8,128)S(1)} %bitcast.74, f32[256,8192]{1,0:T(8,128)} %all-gather.3.cloned.1.call-done), kind=kOutput, calls=%fused_computation.168 | convolution fusion | flops 1610612736 | bytes 10551296 | tf_op jit(solution)/shard_map/dot_general | solution.py:43
  403.6 14.7 %all-gather = f32[512,256]{1,0:T(8,128)S(1)} all-gather(f32[64,256]{1,0:T(8,128)S(1)} %fusion.96), channel_id=2, replica_groups=mesh['grid'=4,'band'=4,'atom'=2] {'grid','atom'}, dimensions={0}, use_global_device_ids=true | all-gather | bytes 589824 | tf_op jit(solution)/shard_map/all_gather | solution.py:108
  418.4 9.1 %all_gather.16 = f32[256,256]{1,0:T(8,128)S(1)} all-gather(f32[64,256]{1,0:T(8,128)S(1)} %broadcast_multiply_fusion), channel_id=1, replica_groups=mesh['grid'=4,'band'=4,'atom'=2] {'band'}, dimensions={0}, use_global_device_ids=true | all-gather | bytes 327680 | tf_op jit(solution)/shard_map/all_gather | solution.py:109
  427.5 0.1 copy.49
  427.7 11.7 %cholesky.50 = f32[128,128]{1,0:T(8,128)S(1)} custom-call(f32[128,128]{1,0:T(8,128)S(1)} %cholesky.118), custom_call_target="Cholesky" | custom-call | tf_op jit(solution)/shard_map/jit(cholesky)/cholesky | solution.py:110
  439.5 9.8 %custom-call.14 = f32[1,128,128]{1,2,0:T(8,128)S(1)} custom-call(f32[1,128,128]{2,1,0:T(8,128)S(1)} %get-tuple-element.55), custom_call_target="InvertDiagBlocksLowerTriangular" | custom-call | tf_op jit(solution)/shard_map/jit(cholesky)/cholesky | solution.py:110
  449.3 0.2 constant_dynamic-update-slice_fusion.3
  449.5 0.3 convolution_subtract_fusion.1
  449.8 11.7 %cholesky.105 = f32[128,128]{1,0:T(8,128)S(1)} custom-call(f32[128,128]{1,0:T(8,128)S(1)} %convolution_subtract_fusion.1), custom_call_target="Cholesky" | custom-call | tf_op jit(solution)/shard_map/jit(cholesky)/cholesky | solution.py:110
  461.5 0.7 compare_reduce_fusion
  462.2 0.6 compare_reduce_fusion.1
  464.2 0.1 triangular_solve.63
  464.2 4.1 while.3
  464.4 0.6 fusion.106
  465.0 1.4 bitcast_dynamic-update-slice_fusion.2
  466.4 0.6 fusion.106
  467.0 1.4 bitcast_dynamic-update-slice_fusion.2
  468.4 19.7 %custom-call.15 = f32[2,128,128]{1,2,0:T(8,128)S(1)} custom-call(f32[2,128,128]{2,1,0:T(8,128)S(1)} %get-tuple-element.36), custom_call_target="InvertDiagBlocksLowerTriangular" | custom-call | tf_op jit(solution)/shard_map/triangular_solve | solution.py:111
  488.1 0.3 fusion.66
  488.3 0.3 convolution_subtract_fusion
  488.6 0.3 fusion.74
  488.9 7.5 %fusion.71 = f32[64,8192]{1,0:T(8,128)S(1)} fusion(f32[256,8192]{1,0:T(8,128)} %all-gather.3.cloned.1.call-done, s32[]{:T(128)S(6)} %select_n.112, f32[128,256]{1,0:T(8,128)S(1)} %fusion.66, f32[128,256]{1,0:T(8,128)S(1)} %fusion.74), kind=kOutput, calls=%fused_computation.114 | convolution fusion | flops 1610629120 | bytes 10747908 | tf_op jit(solution)/shard_map/dot_general | solution.py:117
  496.4 2.5 copy.58
  (40 shorter events, 0.4 us)
Async XLA Ops:
  6.5 126.8 %copy-start = (f32[32,4,512]{2,1,0:T(4,128)S(1)}, f32[32,4,512]{2,1,0:T(4,128)}, u32[]{:S(2)}) copy-start(f32[32,4,512]{2,1,0:T(4,128)} %param.12) | copy-start | bytes 786436
  6.5 280.7 %reduce-scatter.2.cloned.1.call-start = ((), (), s32[]{:S(2)}) async-start(), calls=%async_computation.1 | async-start | bytes 6291456 | tf_op jit(solution)/shard_map/reduce_scatter | solution.py:101
  10.2 6.4 %copy-start.5 = (s32[32,512]{1,0:T(8,128)S(1)}, s32[32,512]{1,0:T(8,128)}, u32[]{:S(2)}) copy-start(s32[32,512]{1,0:T(8,128)} %param.14) | copy-start | bytes 196612
  10.2 7.2 %copy-start.6 = (f32[32,4]{0,1:T(4,128)S(1)}, f32[32,4]{0,1:T(4,128)}, u32[]{:S(2)}) copy-start(f32[32,4]{0,1:T(4,128)} %param.13) | copy-start | bytes 1540
  10.2 40.5 %collective-permute-start = (f32[64,6,1024]{2,0,1:T(8,128)S(1)}, f32[64,6,1024]{2,0,1:T(8,128)}, u32[]{:S(2)}, u32[]{:S(2)}) collective-permute-start(f32[64,6,1024]{2,0,1:T(8,128)S(1)} %copy.60), channel_id=1, source_target_pairs={{0,8},{8,16},{16,24},{24,0},{1,9},{9,17},{17,25},{25,1},{2,10},{10... | collective-permute-start | bytes 4718600 | tf_op jit(solution)/shard_map/ppermute | solution.py:36
  14.2 69.3 %collective-permute-start.1 = (f32[64,6,1024]{2,0,1:T(8,128)S(1)}, f32[64,6,1024]{2,0,1:T(8,128)}, u32[]{:S(2)}, u32[]{:S(2)}) collective-permute-start(f32[64,6,1024]{2,0,1:T(8,128)S(1)} %copy.61), channel_id=1, source_target_pairs={{8,0},{16,8},{24,16},{0,24},{9,1},{17,9},{25,17},{1,25},{10,2},{18... | collective-permute-start | bytes 4718600 | tf_op jit(solution)/shard_map/ppermute | solution.py:37
  201.3 46.7 %collective-permute-start.2 = (f32[64,6,1024]{2,0,1:T(8,128)}, f32[64,6,1024]{2,0,1:T(8,128)}, u32[]{:S(2)}, u32[]{:S(2)}) collective-permute-start(f32[64,6,1024]{2,0,1:T(8,128)} %copy.52), channel_id=1, source_target_pairs={{24,0},{0,8},{8,16},{16,24},{25,1},{1,9},{9,17},{17,25},{26,2},{2,... | collective-permute-start | bytes 4718600 | tf_op jit(solution)/shard_map/ppermute | solution.py:26
  205.1 68.4 %collective-permute-start.3 = (f32[64,6,1024]{2,0,1:T(8,128)}, f32[64,6,1024]{2,0,1:T(8,128)}, u32[]{:S(2)}, u32[]{:S(2)}) collective-permute-start(f32[64,6,1024]{2,0,1:T(8,128)} %copy.53), channel_id=1, source_target_pairs={{8,0},{16,8},{24,16},{0,24},{9,1},{17,9},{25,17},{1,25},{10,2},{18... | collective-permute-start | bytes 4718600 | tf_op jit(solution)/shard_map/ppermute | solution.py:26
  225.1 22.8 %copy-start.3 = (f32[64,6,1024]{2,0,1:T(8,128)S(1)}, f32[64,6,1024]{2,0,1:T(8,128)}, u32[]{:S(2)}) copy-start(f32[64,6,1024]{2,0,1:T(8,128)} %copy.51) | copy-start | bytes 4718596
  276.9 116.6 %all-gather.3.cloned.1.call-start = ((), (), s32[]{:S(2)}) async-start(), calls=%async_computation.2 | async-start | bytes 10485760 | tf_op jit(solution)/shard_map/all_gather | solution.py:107
  277.0 10.3 %copy-start.4 = (f32[8,1024]{1,0:T(8,128)S(1)}, f32[8,1024]{1,0:T(8,128)}, u32[]{:S(2)}) copy-start(f32[8,1024]{1,0:T(8,128)} %param.11) | copy-start | bytes 98308
  304.5 89.0 %copy-start.2 = (f32[8,8,8,1024]{3,2,0,1:T(8,128)S(1)}, f32[8,8,8,1024]{3,2,0,1:T(8,128)}, u32[]{:S(2)}) copy-start(f32[8,8,8,1024]{3,2,0,1:T(8,128)} %copy.55) | copy-start | bytes 6291460
  496.4 2.5 copy-start.1
Sparse Core Ops, SparseCore 0:
  277.0 10.2 reduce-scatter.1
  304.7 88.7 all-gather.2
